TPU v7x, 128 devices: a whole 4x4x4 slice. The times are simulated.
128 devices in a mesh: wide: 16 (over y, z), narrow: 8 (over x, core).
Axes of the slice: x: 4, y: 4, z: 4, core: 2. Of those that a mesh axis runs over, the one named last changes fastest.
Arguments:
- cold_table: float32 [131072, 512], P(('wide', 'narrow')), may hold values from -1.5 to 1.5
- cold_accum: float32 [131072], P(('wide', 'narrow')), may hold values from 0.01 to 1
- hot_table: float32 [2048, 512], replicated, may hold values from -1.5 to 1.5
- hot_accum: float32 [2048], replicated, may hold values from 0.01 to 1
- rel_table: float32 [2048, 512], replicated, may hold values from -3 to 3
- rel_accum: float32 [2048], replicated, may hold values from 0.01 to 1
- req_rows: int32 [128, 768], P(('wide', 'narrow')), may hold values from -1 to 1023, as said below
- head_slot: int32 [32768], P(('wide', 'narrow')), may hold values from 0 to 767, as said below
- tail_slot: int32 [32768], P(('wide', 'narrow')), may hold values from 0 to 767, as said below
- rel_ids: int32 [32768], P(('wide', 'narrow')), may hold values from 0 to 1023
- neg_ids: int32 [128, 1024], P(('wide', 'narrow')), may hold values from 0 to 2047
Outputs:
- new_cold: float32 [131072, 512], P(('wide', 'narrow'))
- new_cold_accum: float32 [131072], P(('wide', 'narrow'))
- new_hot: float32 [2048, 512], replicated
- new_hot_accum: float32 [2048], replicated
- new_rel: float32 [2048, 512], replicated
- new_rel_accum: float32 [2048], replicated
Inputs may be any that keep to these rules, and one draw needn't show every extreme that they name: `req_rows`: in each block of 6 slots of one owner the used slots come first and name distinct rows of that owner; unused slots hold -1; every device uses all 6 slots of some owner. `head_slot`: always a used slot of req_rows of the same device; the owner is slot // 6. `tail_slot`: always a used slot of req_rows of the same device; the owner is slot // 6.
All inputs are finite; a program needn't handle non-finite values.
Results may differ from a plain program's by a relative error of at most 0.00075.
The roundings to bfloat16 on the way count: a program that leaves them out, or rounds other values in their place, can miss the bound.
Values may be sent and summed in bfloat16 or wider, within the bound.
A program may use at most 128 MiB of HBM per device.

v0:
```python
import jax
import jax.numpy as jnp
from jax import lax
from jax.sharding import PartitionSpec as P

REL = 1024
HOT = 2048


def device_terms(head, tail, rel_fwd, rel_inv, negatives):
    queries = jnp.concatenate([head * rel_fwd, tail * rel_inv], axis=0)
    targets = jnp.concatenate([tail, head], axis=0)
    positive = jnp.sum(queries * targets.astype(jnp.float32), axis=-1)
    query_low = queries.astype(jnp.bfloat16)
    scores = jnp.dot(query_low, negatives.T, preferred_element_type=jnp.float32)
    top = jnp.maximum(jnp.max(scores, axis=-1), positive)
    ex_neg = jnp.exp(scores - top[:, None])
    ex_pos = jnp.exp(positive - top)
    total = ex_pos + jnp.sum(ex_neg, axis=-1)
    d_pos = ex_pos / total - 1.0
    p_low = (ex_neg / total[:, None]).astype(jnp.bfloat16)
    d_query = d_pos[:, None] * targets.astype(jnp.float32) + jnp.dot(
        p_low, negatives, preferred_element_type=jnp.float32
    )
    d_target = d_pos[:, None] * queries
    d_negatives = jnp.dot(p_low.T, query_low, preferred_element_type=jnp.float32)
    half = head.shape[0]
    d_head = d_query[:half] * rel_fwd + d_target[half:]
    d_tail = d_query[half:] * rel_inv + d_target[:half]
    d_fwd = d_query[:half] * head.astype(jnp.float32)
    d_inv = d_query[half:] * tail.astype(jnp.float32)
    return (d_head, d_tail, d_fwd, d_inv, d_negatives)


def adagrad(table, accum, grad):
    new_acc = accum + jnp.mean(grad * grad, axis=-1)
    return (table - 0.1 * grad / jnp.sqrt(new_acc + 1e-06)[:, None], new_acc)


def on_device(
    cold_table,
    cold_accum,
    hot_table,
    hot_accum,
    rel_table,
    rel_accum,
    req_rows,
    head_slot,
    tail_slot,
    rel_ids,
    neg_ids,
):
    n_wide = lax.axis_size("wide")
    n_narrow = lax.axis_size("narrow")
    n_dev = n_wide * n_narrow
    rows_own, width = cold_table.shape
    slots_per = req_rows.shape[1] // n_dev
    wanted = req_rows.reshape(n_dev, slots_per)
    asked = lax.all_to_all(wanted, ("wide", "narrow"), split_axis=0, concat_axis=0, tiled=True)
    safe_rows = jnp.maximum(asked, 0).reshape(-1)
    served = cold_table[safe_rows].astype(jnp.bfloat16).reshape(n_dev, slots_per, width)
    fetched = lax.all_to_all(served, ("wide", "narrow"), split_axis=0, concat_axis=0, tiled=True)
    slot_rows = fetched.reshape(n_dev * slots_per, width)
    head = slot_rows[head_slot]
    tail = slot_rows[tail_slot]
    rel_fwd = rel_table[rel_ids]
    rel_inv = rel_table[rel_ids + REL]
    negatives = hot_table[neg_ids[0]].astype(jnp.bfloat16)
    d_head, d_tail, d_fwd, d_inv, d_neg = device_terms(head, tail, rel_fwd, rel_inv, negatives)
    slot_grad = jax.ops.segment_sum(
        jnp.concatenate([d_head, d_tail], axis=0),
        jnp.concatenate([head_slot, tail_slot]),
        num_segments=n_dev * slots_per,
    )
    rel_grad = jax.ops.segment_sum(
        jnp.concatenate([d_fwd, d_inv], axis=0),
        jnp.concatenate([rel_ids, rel_ids + REL]),
        num_segments=2 * REL,
    )
    hot_grad = jax.ops.segment_sum(d_neg, neg_ids[0], num_segments=HOT)
    outgoing = slot_grad.reshape(n_dev, slots_per, width)
    returned = lax.all_to_all(outgoing, ("wide", "narrow"), split_axis=0, concat_axis=0, tiled=True)
    cold_grad = jax.ops.segment_sum(returned.reshape(-1, width), safe_rows, num_segments=rows_own)
    new_cold, new_cold_accum = adagrad(cold_table, cold_accum, cold_grad)
    hot_sum, rel_sum = lax.psum((hot_grad, rel_grad), ("wide", "narrow"))
    new_hot, new_hot_accum = adagrad(hot_table, hot_accum, hot_sum)
    new_rel, new_rel_accum = adagrad(rel_table, rel_accum, rel_sum)
    return (new_cold, new_cold_accum, new_hot, new_hot_accum, new_rel, new_rel_accum)


def solution(mesh):
    in_specs = (
        P(("wide", "narrow"), None),
        P(("wide", "narrow")),
        P(),
        P(),
        P(),
        P(),
        P(("wide", "narrow"), None),
        P(("wide", "narrow")),
        P(("wide", "narrow")),
        P(("wide", "narrow")),
        P(("wide", "narrow"), None),
    )
    out_specs = (P(("wide", "narrow"), None), P(("wide", "narrow")), P(), P(), P(), P())
    return jax.shard_map(
        on_device, mesh=mesh, in_specs=in_specs, out_specs=out_specs, check_vma=False
    )
```

profile of v0, /device:TPU:1, one launch (start us, length us, event | category | flops | bytes accessed | tf_op | source)
XLA Modules:
  0.0 296.1 jit_solution(12856072491615876128)
XLA Ops:
  8.6 11.5 %all-to-all-start = ((s32[128,1,6]{2,1,0:T(1,128)}), s32[128,1,6]{2,1,0:T(1,128)S(1)}, u32[]{:S(2)}, u32[]{:S(2)}) async-start(s32[128,1,6]{2,1,0:T(1,128)} %bitcast), calls=%async_computation | async-start | bytes 131072 | tf_op jit(solution)/shard_map/all_to_all | solution.py:59
  21.5 3.4 %gather_fusion.4 = f32[256,512]{1,0:T(8,128)S(1)} fusion(f32[2048,512]{1,0:T(8,128)} %param.15, s32[1024]{0:T(1024)S(1)} %get-tuple-element.27), kind=kCustom, calls=%fused_computation.4 | custom fusion | bytes 1049600 | tf_op jit(solution)/shard_map/gather | solution.py:67
  24.9 4.2 %gather_fusion.2 = f32[256,512]{1,0:T(8,128)} fusion(f32[2048,512]{1,0:T(8,128)} %param.15, s32[1024]{0:T(1024)S(1)} %get-tuple-element.28), kind=kCustom, calls=%fused_computation.2 | custom fusion | bytes 1049600 | tf_op jit(solution)/shard_map/gather | solution.py:66
  29.1 7.4 %gather_fusion.5 = bf16[1024,512]{1,0:T(8,128)(2,1)} fusion(f32[2048,512]{1,0:T(8,128)} %param.13, s32[1024]{0:T(1024)S(1)} %broadcast_clamp_fusion), kind=kCustom, calls=%fused_computation.5 | custom fusion | bytes 2101248 | tf_op jit(solution)/shard_map/gather | solution.py:68
  36.9 2.1 gather_fusion
  40.3 10.2 %all-to-all-start.1 = ((bf16[128,6,512]{2,1,0:T(8,128)(2,1)}), bf16[128,6,512]{2,1,0:T(8,128)(2,1)}, u32[]{:S(2)}, u32[]{:S(2)}) async-start(bf16[128,6,512]{2,1,0:T(8,128)(2,1)} %convert_element_type.29), calls=%async_computation.1 | async-start | bytes 2097152 | tf_op jit(solution)/shard_map/all_to_all | solution.py:62
  50.9 18.5 %all-to-all-done.1 = bf16[128,6,512]{2,1,0:T(8,128)(2,1)} async-done(((bf16[128,6,512]{2,1,0:T(8,128)(2,1)}), bf16[128,6,512]{2,1,0:T(8,128)(2,1)}, u32[]{:S(2)}, u32[]{:S(2)}) %all-to-all-start.1) | async-done | bytes 786464 | tf_op jit(solution)/shard_map/all_to_all | solution.py:62
  70.8 1.8 gather_fusion.3
  72.7 1.9 gather_fusion.1
  79.8 2.1 fusion.21
  81.9 1.7 convert_multiply_fusion.4
  83.5 9.5 %scatter_custom_fusion.2 = f32[2048,512]{1,0:T(8,128)} fusion(s32[1024]{0:T(1024)} %bitcast.10, f32[1024,512]{1,0:T(8,128)} %fusion.21, f32[]{:T(128)} %constant.11.clone.1), kind=kCustom, calls=%fused_computation.16 | custom fusion | flops 524288 | bytes 4194816 | tf_op jit(solution)/shard_map/scatter-add | solution.py:80
  93.0 5.9 %scatter_custom_fusion.3 = f32[2048,512]{1,0:T(8,128)} fusion(s32[512]{0:T(512)S(1)} %pad_add_fusion.1, f32[]{:T(128)} %constant.11.clone.1, f32[256,512]{1,0:T(8,128)S(1)} %copy-done.12, f32[]{:T(128)} %constant.17.clone.1, f32[256,512]{1,0:T(8,128)S(1)} %copy-done.11), kind=kCustom, calls=%fused_computation.14 | custom fusion | flops 524288 | bytes 5242888 | tf_op jit(solution)/shard_map/scatter-add | solution.py:75
  100.1 4.9 %scatter_custom_fusion = f32[768,512]{1,0:T(8,128)} fusion(s32[512]{0:T(512)S(1)} %pad_add_fusion, f32[256,512]{1,0:T(8,128)S(1)} %copy-done.9, f32[]{:T(128)} %constant.17.clone.1, f32[256,512]{1,0:T(8,128)S(1)} %copy-done.10, f32[]{:T(128)} %constant.11.clone.1), kind=kCustom, calls=%fused_computation.28 | custom fusion | flops 524288 | bytes 2621448 | tf_op jit(solution)/shard_map/scatter-add | solution.py:70
  105.1 2.6 reshape.97
  107.7 39.4 %all_to_all.19 = f32[128,6,512]{2,1,0:T(8,128)} all-to-all(f32[128,6,512]{2,1,0:T(8,128)} %reshape.97), channel_id=1, replica_groups=mesh['wide'=16,'narrow'=8] {'wide','narrow'}, dimensions={0} | all-to-all | bytes 3145728 | tf_op jit(solution)/shard_map/all_to_all | solution.py:82
  147.1 2.6 reshape.159
  149.7 8.7 %scatter_custom_fusion.1 = f32[1024,512]{1,0:T(8,128)} fusion(s32[768]{0:T(1024)S(1)} %reshape.157, f32[768,512]{1,0:T(8,128)} %reshape.159, f32[]{:T(128)} %constant.11.clone.1), kind=kCustom, calls=%fused_computation.35 | custom fusion | flops 393216 | bytes 2097664 | tf_op jit(solution)/shard_map/scatter-add | solution.py:83
  158.4 2.0 multiply_reduce_fusion.2
  161.0 1.7 divide_subtract_fusion.2
  162.7 113.1 %all-reduce.3.cloned.1.call-done = (f32[2048,512]{1,0:T(8,128)}, f32[2048,512]{1,0:T(8,128)}) async-done(((f32[2048,512]{1,0:T(8,128)}, f32[2048,512]{1,0:T(8,128)}), (f32[2048,512]{1,0:T(8,128)}, f32[2048,512]{1,0:T(8,128)})) %all-reduce.3.cloned.1.call-update) | async-done | bytes 8388624 | tf_op jit(solution)/shard_map/psum | solution.py:85
  275.8 2.7 multiply_reduce_fusion
  279.3 5.1 %divide_subtract_fusion = f32[2048,512]{1,0:T(8,128)} fusion(f32[2048,512]{1,0:T(8,128)S(1)} %copy-done, f32[2048,512]{1,0:T(8,128)} %get-tuple-element.7, f32[2048]{0:T(1024)S(1)} %get-tuple-element.8), kind=kLoop, calls=%fused_computation.10 | loop fusion | flops 3145728 | bytes 12591104 | tf_op jit(solution)/shard_map/sub | solution.py:37
  286.6 2.7 divide_subtract_fusion.1
  (72 shorter events, 16.0 us)
Async XLA Ops:
  8.6 27.9 %all-to-all-start = ((s32[128,1,6]{2,1,0:T(1,128)}), s32[128,1,6]{2,1,0:T(1,128)S(1)}, u32[]{:S(2)}, u32[]{:S(2)}) async-start(s32[128,1,6]{2,1,0:T(1,128)} %bitcast), calls=%async_computation | async-start | bytes 131072 | tf_op jit(solution)/shard_map/all_to_all | solution.py:59
  29.1 7.8 %copy-start.2 = (f32[1024,512]{1,0:T(8,128)S(1)}, f32[1024,512]{1,0:T(8,128)}, u32[]{:S(2)}) copy-start(f32[1024,512]{1,0:T(8,128)} %param.11) | copy-start | bytes 6291460
  39.1 11.7 %copy-start.18 = (s32[256]{0:T(256)S(1)}, s32[256]{0:T(256)}, u32[]{:S(2)}) copy-start(s32[256]{0:T(256)} %param.20) | copy-start | bytes 3076
  39.1 11.7 %copy-start.15 = (s32[256]{0:T(256)S(1)}, s32[256]{0:T(256)}, u32[]{:S(2)}) copy-start(s32[256]{0:T(256)} %param.19) | copy-start | bytes 3076
  39.1 11.8 %copy-start.16 = (s32[256]{0:T(256)S(1)}, s32[256]{0:T(256)}, u32[]{:S(2)}) copy-start(s32[256]{0:T(256)} %param.18) | copy-start | bytes 3076
  40.3 29.1 %all-to-all-start.1 = ((bf16[128,6,512]{2,1,0:T(8,128)(2,1)}), bf16[128,6,512]{2,1,0:T(8,128)(2,1)}, u32[]{:S(2)}, u32[]{:S(2)}) async-start(bf16[128,6,512]{2,1,0:T(8,128)(2,1)} %convert_element_type.29), calls=%async_computation.1 | async-start | bytes 2097152 | tf_op jit(solution)/shard_map/all_to_all | solution.py:62
  50.5 225.3 %all-reduce.3.cloned.1.call-start = ((), (), s32[]{:S(2)}) async-start(), calls=%async_computation.3 | async-start | bytes 16777216 | tf_op jit(solution)/shard_map/psum | solution.py:85
  74.5 2.3 copy-start.6
  74.5 2.3 copy-start.7
  74.5 2.6 copy-start.8
  79.8 2.1 copy-start.5
  83.5 9.5 %copy-start.11 = (f32[256,512]{1,0:T(8,128)S(1)}, f32[256,512]{1,0:T(8,128)}, u32[]{:S(2)}) copy-start(f32[256,512]{1,0:T(8,128)} %get-tuple-element.16) | copy-start | bytes 1572868
  83.5 9.5 %copy-start.12 = (f32[256,512]{1,0:T(8,128)S(1)}, f32[256,512]{1,0:T(8,128)}, u32[]{:S(2)}) copy-start(f32[256,512]{1,0:T(8,128)} %get-tuple-element.17) | copy-start | bytes 1572868
  98.9 1.0 copy-start.9
  98.9 1.2 copy-start.10
  149.7 10.6 %copy-start.17 = (f32[1024]{0:T(1024)S(1)}, f32[1024]{0:T(1024)}, u32[]{:S(2)}) copy-start(f32[1024]{0:T(1024)} %param.12) | copy-start | bytes 12292
  158.4 2.6 copy-start.3
  275.8 2.7 copy-start.13
  275.8 3.5 %copy-start = (f32[2048,512]{1,0:T(8,128)S(1)}, f32[2048,512]{1,0:T(8,128)}, u32[]{:S(2)}) copy-start(f32[2048,512]{1,0:T(8,128)} %param.15) | copy-start | bytes 12582916
  279.3 5.1 %copy-start.4 = (f32[2048,512]{1,0:T(8,128)S(1)}, f32[2048,512]{1,0:T(8,128)}, u32[]{:S(2)}) copy-start(f32[2048,512]{1,0:T(8,128)} %get-tuple-element.6) | copy-start | bytes 12582916
  284.3 0.7 copy-start.14
  284.3 2.2 copy-start.1
Sparse Core Ops, SparseCore 0:
  99.1 176.6 all-reduce.2
where the time goes:
time: 297 us; the launch traced here: 296 us
  waiting for transfers between devices  132 us (44%)
  other arithmetic  52.9 us (18%)
  blocking collectives  39.4 us (13%)
  local copies, waits for them, and re-layouts  32.2 us (11%)
  starting transfers between devices  21.9 us (7%)
  between operations  14.3 us (5%)
  matrix products  3.65 us (1%)
    psum x1, waiting for transfers between devices, on_device(): hot_sum, rel_sum = lax.psum((hot_grad, rel_grad), ('wide', 'narrow'))  113 us
    all_to_all x1, blocking collectives, on_device(): lax.all_to_all(outgoing, ('wide', 'narrow'), split_axis=0, concat_axis=0,...  39.4 us
    all_to_all x1, waiting for transfers between devices, on_device(): lax.all_to_all(served, ('wide', 'narrow'), split_axis=0, concat_axis=0, t...  18.5 us
    all_to_all x1, starting transfers between devices, on_device(): lax.all_to_all(wanted, ('wide', 'narrow'), split_axis=0, concat_axis=0, t...  11.5 us
    all_to_all x1, starting transfers between devices, on_device(): lax.all_to_all(served, ('wide', 'narrow'), split_axis=0, concat_axis=0, t...  10.2 us
    scatter-add x1, other arithmetic, on_device(): hot_grad = jax.ops.segment_sum(d_neg, neg_ids[0], num_segments=HOT)  9.52 us
    sub x3, other arithmetic, adagrad(): return (table - 0.1 * grad / jnp.sqrt(new_acc + 1e-06)[:, None], new_acc)  9.49 us
    scatter-add x1, other arithmetic, on_device(): jax.ops.segment_sum(returned.reshape(-1, width), safe_rows, num_segments=...  8.67 us
  transfers between devices with their start and end apart: 3, of which 2 were waited for; matrix products, arithmetic and copies ran while one was open for 13% of the time, Pallas kernels for 0%

commit v1 on v0

--- a/solution.py
+++ b/solution.py
@@ -1,10 +1,183 @@
+import functools
 import jax
 import jax.numpy as jnp
 from jax import lax
+from jax.experimental import pallas as pl
+from jax.experimental.pallas import tpu as pltpu
 from jax.sharding import PartitionSpec as P
 
 REL = 1024
 HOT = 2048
+MESH = pl.DeviceIdType.MESH
+F32 = jnp.float32
+BF16 = jnp.bfloat16
+ROT = ((0, 1, 2), (1, 2, 0), (2, 0, 1))
+UNIT_ROT = (0, 0, 1, 2, 1, 1, 2, 2)
+LANES = 128
+
+
+def place():
+    wide = lax.axis_index("wide")
+    narrow = lax.axis_index("narrow")
+    return (narrow // 2, wide // 4, wide % 4), narrow % 2
+
+
+def device(coords, core):
+    x, y, z = coords
+    return (y * 4 + z, x * 2 + core)
+
+
+def shifted(coords, axis, step):
+    out = list(coords)
+    out[axis] = (out[axis] + step) % 4
+    return tuple(out)
+
+
+def reduce_kernel(hot_ref, rel_ref, hot_out, rel_out, hot_pair, rel_pair, hot_sum, rel_sum, rel_low,
+                  hot_r1, rel_r1, acc1, r2, acc2, r3, psend, precv, send, recv):
+    coords, core = place()
+    mate = device(coords, 1 - core)
+    rows = HOT // 2
+
+    barrier = pltpu.get_barrier_semaphore()
+    pl.semaphore_signal(barrier, inc=1, device_id=mate, device_id_type=MESH)
+    for axis in range(3):
+        for step in (1, 2, 3):
+            pl.semaphore_signal(barrier, inc=1, device_id=device(shifted(coords, axis, step), core), device_id_type=MESH)
+    pl.semaphore_wait(barrier, 10)
+
+    mine = pl.ds(pl.multiple_of(core * rows, rows), rows)
+    other = pl.ds(pl.multiple_of((1 - core) * rows, rows), rows)
+    pairs = []
+    for k, (src, dst) in enumerate(((hot_ref, hot_pair), (rel_ref, rel_pair))):
+        c = pltpu.make_async_remote_copy(src_ref=src.at[other], dst_ref=dst, send_sem=psend.at[k], recv_sem=precv.at[k],
+                                         device_id=mate, device_id_type=MESH)
+        c.start()
+        pairs.append(c)
+
+    def low(u):
+        return u >= 4
+
+    def cols(u):
+        return slice((u % 4) * LANES, (u % 4 + 1) * LANES)
+
+    def idx(u):
+        r = ROT[UNIT_ROT[u]]
+        return r, [coords[a] for a in r]
+
+    def block(start, size):
+        return pl.ds(pl.multiple_of(start, 16), size)
+
+    copies = []
+
+    def send_to(phase, u, axis, step, src, dst):
+        c = pltpu.make_async_remote_copy(src_ref=src, dst_ref=dst, send_sem=send.at[phase, u, step - 1], recv_sem=recv.at[phase, u, step - 1],
+                                         device_id=device(shifted(coords, axis, step), core), device_id_type=MESH)
+        c.start()
+        copies.append(c)
+        return c
+
+    phase1 = {}
+    for k in range(2):
+        pairs[k].wait_recv()
+        if k == 0:
+            hot_sum[...] = hot_ref[mine, :] + hot_pair[...]
+        else:
+            total = rel_ref[mine, :] + rel_pair[...]
+            rel_sum[...] = total
+            rel_low[...] = total.astype(BF16)
+        for u in range(4 * k, 4 * k + 4):
+            r, i = idx(u)
+            src, dst = (rel_low, rel_r1.at[u - 4]) if low(u) else (hot_sum, hot_r1.at[u])
+            for step in (1, 2, 3):
+                j = (i[0] + step) % 4
+                phase1[u, step] = send_to(0, u, r[0], step, src.at[block(j * 256, 256), cols(u)], dst.at[step - 1])
+    phase2 = {}
+    for u in range(8):
+        r, i = idx(u)
+        for step in (1, 2, 3):
+            phase1[u, step].wait_recv()
+        own = (rel_sum if low(u) else hot_sum)[block(i[0] * 256, 256), cols(u)]
+        got = rel_r1[u - 4] if low(u) else hot_r1[u]
+        acc1[u] = own + (got[0].astype(F32) + got[1].astype(F32) + got[2].astype(F32))
+        for step in (1, 2, 3):
+            j = (i[1] + step) % 4
+            phase2[u, step] = send_to(1, u, r[1], step, acc1.at[u, block(j * 64, 64)], r2.at[u, step - 1])
+    phase3 = {}
+    for u in range(8):
+        r, i = idx(u)
+        for step in (1, 2, 3):
+            phase2[u, step].wait_recv()
+        acc2[u] = acc1[u, block(i[1] * 64, 64), :] + (r2[u, 0] + r2[u, 1] + r2[u, 2])
+        for step in (1, 2, 3):
+            j = (i[2] + step) % 4
+            phase3[u, step] = send_to(2, u, r[2], step, acc2.at[u, block(j * 16, 16)], r3.at[u, step - 1])
+
+    base = core * rows
+    gathers = {}
+
+    def gather(phase, u, level):
+        r, i = idx(u)
+        start = base
+        size = 1024
+        for a in range(level + 1):
+            size //= 4
+            start = start + i[a] * size
+        out = rel_out if low(u) else hot_out
+        ref = out.at[block(start, size), cols(u)]
+        for step in (1, 2, 3):
+            gathers[phase, u, step] = send_to(phase, u, r[level], step, ref, ref)
+
+    for u in range(8):
+        r, i = idx(u)
+        for step in (1, 2, 3):
+            phase3[u, step].wait_recv()
+        total = acc2[u, block(i[2] * 16, 16), :] + (r3[u, 0] + r3[u, 1] + r3[u, 2])
+        out = rel_out if low(u) else hot_out
+        start = base + i[0] * 256 + i[1] * 64 + i[2] * 16
+        out[block(start, 16), cols(u)] = total.astype(out.dtype)
+        gather(3, u, 2)
+    for level in (1, 0):
+        for u in range(8):
+            for step in (1, 2, 3):
+                gathers[4 - level, u, step].wait_recv()
+            gather(5 - level, u, level)
+    last = []
+    for u in range(8):
+        for step in (1, 2, 3):
+            gathers[5, u, step].wait_recv()
+        out = rel_out if low(u) else hot_out
+        ref = out.at[mine, cols(u)]
+        c = pltpu.make_async_remote_copy(src_ref=ref, dst_ref=ref, send_sem=psend.at[2 + u], recv_sem=precv.at[2 + u],
+                                         device_id=mate, device_id_type=MESH)
+        c.start()
+        last.append(c)
+    for c in last:
+        c.wait_recv()
+    for c in pairs + copies + last:
+        c.wait_send()
+
+
+def all_sum(hot_grad, rel_grad):
+    width = hot_grad.shape[1]
+    vmem = pl.BlockSpec(memory_space=pltpu.VMEM)
+    half = HOT // 2
+    return pl.pallas_call(
+        reduce_kernel,
+        out_shape=(jax.ShapeDtypeStruct((HOT, width), F32), jax.ShapeDtypeStruct((2 * REL, width), BF16)),
+        in_specs=[vmem, vmem],
+        out_specs=(vmem, vmem),
+        scratch_shapes=[
+            pltpu.VMEM((half, width), F32), pltpu.VMEM((half, width), F32),
+            pltpu.VMEM((half, width), F32), pltpu.VMEM((half, width), F32), pltpu.VMEM((half, width), BF16),
+            pltpu.VMEM((4, 3, 256, LANES), F32), pltpu.VMEM((4, 3, 256, LANES), BF16),
+            pltpu.VMEM((8, 256, LANES), F32), pltpu.VMEM((8, 3, 64, LANES), F32),
+            pltpu.VMEM((8, 64, LANES), F32), pltpu.VMEM((8, 3, 16, LANES), F32),
+            pltpu.SemaphoreType.DMA((10,)), pltpu.SemaphoreType.DMA((10,)),
+            pltpu.SemaphoreType.DMA((6, 8, 3)), pltpu.SemaphoreType.DMA((6, 8, 3)),
+        ],
+        compiler_params=pltpu.CompilerParams(collective_id=0, has_side_effects=True, vmem_limit_bytes=60 << 20),
+    )(hot_grad, rel_grad)
 
 
 def device_terms(head, tail, rel_fwd, rel_inv, negatives):
@@ -82,9 +255,9 @@
     returned = lax.all_to_all(outgoing, ("wide", "narrow"), split_axis=0, concat_axis=0, tiled=True)
     cold_grad = jax.ops.segment_sum(returned.reshape(-1, width), safe_rows, num_segments=rows_own)
     new_cold, new_cold_accum = adagrad(cold_table, cold_accum, cold_grad)
-    hot_sum, rel_sum = lax.psum((hot_grad, rel_grad), ("wide", "narrow"))
+    hot_sum, rel_sum = all_sum(hot_grad, rel_grad)
     new_hot, new_hot_accum = adagrad(hot_table, hot_accum, hot_sum)
-    new_rel, new_rel_accum = adagrad(rel_table, rel_accum, rel_sum)
+    new_rel, new_rel_accum = adagrad(rel_table, rel_accum, rel_sum.astype(F32))
     return (new_cold, new_cold_accum, new_hot, new_hot_accum, new_rel, new_rel_accum)
 
 

time: 297 us -> 219 us (0.74)
  waiting for transfers between devices: 132 us -> 38.1 us
  Pallas kernels: 0 us -> 61.8 us
  blocking collectives: 39.4 us -> 0 us
  between operations: 14.3 us -> 0.92 us
  starting transfers between devices: 21.9 us -> 27.3 us
  other arithmetic: 52.9 us -> 56 us
    psum x1 -> x0, waiting for transfers between devices: 113 us -> none  [on_device(): hot_sum, rel_sum = lax.psum((hot_grad, rel_grad), ('wide', 'narrow'))]
    pallas_call x0 -> x1, Pallas kernels: none -> 61.8 us  [all_sum(): pl.pallas_call(reduce_kernel, out_shape=(jax.ShapeDtypeStruct((HOT, width...]
    all_to_all x1 -> x0, blocking collectives: 39.4 us -> none  [on_device(): lax.all_to_all(outgoing, ('wide', 'narrow'), split_axis=0, concat_axis=0,...]
    all_to_all x0 -> x1, waiting for transfers between devices: none -> 19.3 us  [on_device(): lax.all_to_all(outgoing, ('wide', 'narrow'), split_axis=0, concat_axis=0,...]
    all_to_all x0 -> x1, starting transfers between devices: none -> 5.54 us  [on_device(): lax.all_to_all(outgoing, ('wide', 'narrow'), split_axis=0, concat_axis=0,...]
  transfers between devices with their start and end apart: 3 -> 3, of which waited for: 2 -> 2; matrix products, arithmetic and copies ran while one was open for 13% -> 12% of each run, Pallas kernels for 0% -> 0%
where the time goes in v1:
time: 219 us; the launch traced here: 218 us
  Pallas kernels  61.8 us (28%)
  other arithmetic  56 us (26%)
  waiting for transfers between devices  38.1 us (17%)
  local copies, waits for them, and re-layouts  30.7 us (14%)
  starting transfers between devices  27.3 us (12%)
  matrix products  3.65 us (2%)
    pallas_call x1, Pallas kernels, all_sum(): pl.pallas_call(reduce_kernel, out_shape=(jax.ShapeDtypeStruct((HOT, width...  61.8 us
    all_to_all x1, waiting for transfers between devices, on_device(): lax.all_to_all(outgoing, ('wide', 'narrow'), split_axis=0, concat_axis=0,...  19.3 us
    all_to_all x1, waiting for transfers between devices, on_device(): lax.all_to_all(served, ('wide', 'narrow'), split_axis=0, concat_axis=0, t...  18.8 us
    all_to_all x1, starting transfers between devices, on_device(): lax.all_to_all(wanted, ('wide', 'narrow'), split_axis=0, concat_axis=0, t...  11.5 us
    all_to_all x1, starting transfers between devices, on_device(): lax.all_to_all(served, ('wide', 'narrow'), split_axis=0, concat_axis=0, t...  10.2 us
    sub x3, other arithmetic, adagrad(): return (table - 0.1 * grad / jnp.sqrt(new_acc + 1e-06)[:, None], new_acc)  10.2 us
    scatter-add x1, other arithmetic, on_device(): hot_grad = jax.ops.segment_sum(d_neg, neg_ids[0], num_segments=HOT)  9.48 us
    scatter-add x1, other arithmetic, on_device(): jax.ops.segment_sum(returned.reshape(-1, width), safe_rows, num_segments=...  8.65 us
  transfers between devices with their start and end apart: 3, of which 2 were waited for; matrix products, arithmetic and copies ran while one was open for 12% of the time, Pallas kernels for 0%

profile of v1, /device:TPU:1, one launch (start us, length us, event | category | flops | bytes accessed | tf_op | source)
XLA Modules:
  0.0 218.5 jit_solution(15059380542385933589)
XLA Ops:
  2.1 11.5 %all-to-all-start = ((s32[128,1,6]{2,1,0:T(1,128)}), s32[128,1,6]{2,1,0:T(1,128)S(1)}, u32[]{:S(2)}, u32[]{:S(2)}) async-start(s32[128,1,6]{2,1,0:T(1,128)} %bitcast), calls=%async_computation | async-start | bytes 131072 | tf_op jit(solution)/shard_map/all_to_all | solution.py:232
  15.7 3.4 %gather_fusion.4 = f32[256,512]{1,0:T(8,128)S(1)} fusion(f32[2048,512]{1,0:T(8,128)} %param.15, s32[1024]{0:T(1024)S(1)} %get-tuple-element.29), kind=kCustom, calls=%fused_computation.4 | custom fusion | bytes 1049600 | tf_op jit(solution)/shard_map/gather | solution.py:240
  19.1 4.2 %gather_fusion.2 = f32[256,512]{1,0:T(8,128)} fusion(f32[2048,512]{1,0:T(8,128)} %param.15, s32[1024]{0:T(1024)S(1)} %get-tuple-element.30), kind=kCustom, calls=%fused_computation.2 | custom fusion | bytes 1049600 | tf_op jit(solution)/shard_map/gather | solution.py:239
  23.3 7.4 %gather_fusion.5 = bf16[1024,512]{1,0:T(8,128)(2,1)} fusion(f32[2048,512]{1,0:T(8,128)} %param.13, s32[1024]{0:T(1024)S(1)} %broadcast_clamp_fusion), kind=kCustom, calls=%fused_computation.5 | custom fusion | bytes 2101248 | tf_op jit(solution)/shard_map/gather | solution.py:241
  31.1 2.1 gather_fusion
  34.5 10.2 %all-to-all-start.1 = ((bf16[128,6,512]{2,1,0:T(8,128)(2,1)}), bf16[128,6,512]{2,1,0:T(8,128)(2,1)}, u32[]{:S(2)}, u32[]{:S(2)}) async-start(bf16[128,6,512]{2,1,0:T(8,128)(2,1)} %convert_element_type.32), calls=%async_computation.1 | async-start | bytes 2097152 | tf_op jit(solution)/shard_map/all_to_all | solution.py:235
  44.8 18.8 %all-to-all-done.1 = bf16[128,6,512]{2,1,0:T(8,128)(2,1)} async-done(((bf16[128,6,512]{2,1,0:T(8,128)(2,1)}), bf16[128,6,512]{2,1,0:T(8,128)(2,1)}, u32[]{:S(2)}, u32[]{:S(2)}) %all-to-all-start.1) | async-done | bytes 786464 | tf_op jit(solution)/shard_map/all_to_all | solution.py:235
  65.0 1.8 gather_fusion.3
  66.8 1.9 gather_fusion.1
  73.9 2.1 fusion.24
  77.4 9.5 %scatter_custom_fusion.2.hot_ref = f32[2048,512]{1,0:T(8,128)} fusion(s32[1024]{0:T(1024)} %bitcast.10, f32[1024,512]{1,0:T(8,128)} %fusion.24, f32[]{:T(128)} %constant.11.clone.1), kind=kCustom, calls=%fused_computation.19 | custom fusion | flops 524288 | bytes 4194816 | tf_op jit(solution)/shard_map/scatter-add | solution.py:253
  86.9 6.4 %scatter_custom_fusion.3.rel_ref = f32[2048,512]{1,0:T(8,128)} fusion(s32[512]{0:T(512)S(1)} %pad_add_fusion.1, f32[]{:T(128)} %constant.11.clone.1, f32[256,512]{1,0:T(8,128)} %get-tuple-element.19, f32[]{:T(128)} %constant.17.clone.1, f32[256,512]{1,0:T(8,128)S(1)} %copy-done.9), kind=kCustom, calls=%fused_computation.17 | custom fusion | flops 524288 | bytes 5242888 | tf_op jit(solution)/shard_map/scatter-add | solution.py:248
  93.3 61.8 %shard_map.154 = (f32[2048,512]{1,0:T(8,128)}, bf16[2048,512]{1,0:T(8,128)(2,1)}) custom-call(f32[2048,512]{1,0:T(8,128)} %scatter_custom_fusion.2.hot_ref, f32[2048,512]{1,0:T(8,128)} %scatter_custom_fusion.3.rel_ref), custom_call_target="tpu_custom_call" | custom-call | tf_op jit(solution)/shard_map/pallas_call | solution.py:165
  155.1 2.1 fusion.2
  157.2 2.6 %multiply_reduce_fusion = f32[2048]{0:T(1024)S(1)} fusion(f32[2048,512]{1,0:T(8,128)} %get-tuple-element.8), kind=kLoop, calls=%fused_computation.16 | loop fusion | flops 2095104 | bytes 4202496 | tf_op jit(solution)/shard_map/reduce_sum | solution.py:209
  159.8 4.8 %scatter_custom_fusion = f32[768,512]{1,0:T(8,128)} fusion(s32[512]{0:T(512)S(1)} %pad_add_fusion, f32[256,512]{1,0:T(8,128)S(1)} %get-tuple-element.20, f32[]{:T(128)} %constant.17.clone.1, f32[256,512]{1,0:T(8,128)S(1)} %copy-done.8, f32[]{:T(128)} %constant.11.clone.1), kind=kCustom, calls=%fused_computation.31 | custom fusion | flops 524288 | bytes 2621448 | tf_op jit(solution)/shard_map/scatter-add | solution.py:243
  164.7 2.6 %reshape.97 = f32[128,6,512]{2,1,0:T(8,128)} reshape(f32[768,512]{1,0:T(8,128)} %scatter_custom_fusion) | data formatting | bytes 3145728 | tf_op jit(solution)/shard_map/reshape | solution.py:254
  167.3 5.5 %all-to-all-start.2 = ((f32[128,6,512]{2,1,0:T(8,128)}), f32[128,6,512]{2,1,0:T(8,128)}, u32[]{:S(2)}, u32[]{:S(2)}) async-start(f32[128,6,512]{2,1,0:T(8,128)} %reshape.97), calls=%async_computation.2 | async-start | bytes 4194304 | tf_op jit(solution)/shard_map/all_to_all | solution.py:255
  174.1 5.8 %fusion.1 = f32[2048,512]{1,0:T(8,128)} fusion(f32[2048,512]{1,0:T(8,128)} %param.15, bf16[2048,512]{1,0:T(8,128)(2,1)} %get-tuple-element.9, f32[2048]{0:T(1024)S(1)} %get-tuple-element.10), kind=kLoop, calls=%fused_computation.13 | loop fusion | flops 4194304 | bytes 10493952 | tf_op jit(solution)/shard_map/sub | solution.py:210
  180.9 2.7 %divide_subtract_fusion = f32[2048,512]{1,0:T(8,128)} fusion(f32[2048,512]{1,0:T(8,128)S(1)} %copy-done, f32[2048,512]{1,0:T(8,128)S(1)} %copy-done.3, f32[2048]{0:T(1024)S(1)} %get-tuple-element.12), kind=kLoop, calls=%fused_computation.15 | loop fusion | flops 3145728 | bytes 12591104 | tf_op jit(solution)/shard_map/sub | solution.py:210
  183.6 19.3 %all-to-all-done.2 = f32[128,6,512]{2,1,0:T(8,128)} async-done(((f32[128,6,512]{2,1,0:T(8,128)}), f32[128,6,512]{2,1,0:T(8,128)}, u32[]{:S(2)}, u32[]{:S(2)}) %all-to-all-start.2) | async-done | bytes 1572896 | tf_op jit(solution)/shard_map/all_to_all | solution.py:255
  202.9 2.6 %reshape.159 = f32[768,512]{1,0:T(8,128)} reshape(f32[128,6,512]{2,1,0:T(8,128)} %all-to-all-done.2) | data formatting | bytes 3145728 | tf_op jit(solution)/shard_map/reshape | solution.py:256
  205.5 8.7 %scatter_custom_fusion.1 = f32[1024,512]{1,0:T(8,128)} fusion(s32[768]{0:T(1024)S(1)} %reshape.157, f32[768,512]{1,0:T(8,128)} %reshape.159, f32[]{:T(128)} %constant.11.clone.1), kind=kCustom, calls=%fused_computation.38 | custom fusion | flops 393216 | bytes 2097664 | tf_op jit(solution)/shard_map/scatter-add | solution.py:256
  214.2 2.0 multiply_reduce_fusion.1
  (63 shorter events, 17.8 us)
Async XLA Ops:
  2.1 28.6 %all-to-all-start = ((s32[128,1,6]{2,1,0:T(1,128)}), s32[128,1,6]{2,1,0:T(1,128)S(1)}, u32[]{:S(2)}, u32[]{:S(2)}) async-start(s32[128,1,6]{2,1,0:T(1,128)} %bitcast), calls=%async_computation | async-start | bytes 131072 | tf_op jit(solution)/shard_map/all_to_all | solution.py:232
  23.3 7.8 %copy-start.1 = (f32[1024,512]{1,0:T(8,128)S(1)}, f32[1024,512]{1,0:T(8,128)}, u32[]{:S(2)}) copy-start(f32[1024,512]{1,0:T(8,128)} %param.11) | copy-start | bytes 6291460
  33.2 11.5 %copy-start.12 = (s32[256]{0:T(256)S(1)}, s32[256]{0:T(256)}, u32[]{:S(2)}) copy-start(s32[256]{0:T(256)} %param.19) | copy-start | bytes 3076
  33.2 11.5 %copy-start.13 = (s32[256]{0:T(256)S(1)}, s32[256]{0:T(256)}, u32[]{:S(2)}) copy-start(s32[256]{0:T(256)} %param.18) | copy-start | bytes 3076
  34.5 29.1 %all-to-all-start.1 = ((bf16[128,6,512]{2,1,0:T(8,128)(2,1)}), bf16[128,6,512]{2,1,0:T(8,128)(2,1)}, u32[]{:S(2)}, u32[]{:S(2)}) async-start(bf16[128,6,512]{2,1,0:T(8,128)(2,1)} %convert_element_type.32), calls=%async_computation.1 | async-start | bytes 2097152 | tf_op jit(solution)/shard_map/all_to_all | solution.py:235
  68.6 2.3 %copy-start.5 = (bf16[256,512]{1,0:T(8,128)(2,1)S(1)}, bf16[256,512]{1,0:T(8,128)(2,1)}, u32[]{:S(2)}) copy-start(bf16[256,512]{1,0:T(8,128)(2,1)} %gather_fusion.3) | copy-start | bytes 786436
  68.7 2.3 %copy-start.6 = (bf16[256,512]{1,0:T(8,128)(2,1)S(1)}, bf16[256,512]{1,0:T(8,128)(2,1)}, u32[]{:S(2)}) copy-start(bf16[256,512]{1,0:T(8,128)(2,1)} %gather_fusion.1) | copy-start | bytes 786436
  68.7 2.6 %copy-start.7 = (bf16[1024,512]{1,0:T(8,128)(2,1)S(1)}, bf16[1024,512]{1,0:T(8,128)(2,1)}, u32[]{:S(2)}) copy-start(bf16[1024,512]{1,0:T(8,128)(2,1)} %gather_fusion.5) | copy-start | bytes 3145732
  73.9 2.1 copy-start.4
  77.4 9.5 %copy-start.9 = (f32[256,512]{1,0:T(8,128)S(1)}, f32[256,512]{1,0:T(8,128)}, u32[]{:S(2)}) copy-start(f32[256,512]{1,0:T(8,128)} %get-tuple-element.18) | copy-start | bytes 1572868
  157.2 2.6 %copy-start.8 = (f32[256,512]{1,0:T(8,128)S(1)}, f32[256,512]{1,0:T(8,128)}, u32[]{:S(2)}) copy-start(f32[256,512]{1,0:T(8,128)} %get-tuple-element.21) | copy-start | bytes 1572868
  167.3 5.6 %copy-start.10 = (f32[2048]{0:T(1024)S(1)}, f32[2048]{0:T(1024)}, u32[]{:S(2)}) copy-start(f32[2048]{0:T(1024)} %param.16) | copy-start | bytes 24580
  167.3 6.2 %copy-start.11 = (f32[2048]{0:T(1024)S(1)}, f32[2048]{0:T(1024)}, u32[]{:S(2)}) copy-start(f32[2048]{0:T(1024)} %param.14) | copy-start | bytes 24580
  167.3 35.6 %all-to-all-start.2 = ((f32[128,6,512]{2,1,0:T(8,128)}), f32[128,6,512]{2,1,0:T(8,128)}, u32[]{:S(2)}, u32[]{:S(2)}) async-start(f32[128,6,512]{2,1,0:T(8,128)} %reshape.97), calls=%async_computation.2 | async-start | bytes 4194304 | tf_op jit(solution)/shard_map/all_to_all | solution.py:255
  174.0 5.8 %copy-start = (f32[2048,512]{1,0:T(8,128)S(1)}, f32[2048,512]{1,0:T(8,128)}, u32[]{:S(2)}) copy-start(f32[2048,512]{1,0:T(8,128)} %param.13) | copy-start | bytes 12582916
  174.0 6.8 %copy-start.3 = (f32[2048,512]{1,0:T(8,128)S(1)}, f32[2048,512]{1,0:T(8,128)}, u32[]{:S(2)}) copy-start(f32[2048,512]{1,0:T(8,128)} %get-tuple-element.8) | copy-start | bytes 12582916
  205.5 10.6 %copy-start.14 = (f32[1024]{0:T(1024)S(1)}, f32[1024]{0:T(1024)}, u32[]{:S(2)}) copy-start(f32[1024]{0:T(1024)} %param.12) | copy-start | bytes 12292
  214.2 2.6 %copy-start.2 = (f32[1024,512]{1,0:T(8,128)S(1)}, f32[1024,512]{1,0:T(8,128)}, u32[]{:S(2)}) copy-start(f32[1024,512]{1,0:T(8,128)} %scatter_custom_fusion.1) | copy-start | bytes 6291460
